TPU v7x, 128 devices: a whole 4x4x4 slice. The times are simulated.
128 devices in a mesh: row: 16 (over x, z), col: 8 (over y, core).
Axes of the slice: x: 4, y: 4, z: 4, core: 2. Of those that a mesh axis runs over, the one named last changes fastest.
Arguments:
- attn: bfloat16 [2048, 16384], P('col', 'row'), may hold values from -6 to 6
- grad_out: bfloat16 [2048, 16384], P('row', 'col'), may hold values from -0.119628906 to 0.119628906
- weight: bfloat16 [16384, 16384], P('row', 'col'), may hold values from -2.09375 to 2.09375
- momentum: bfloat16 [16384, 16384], P('row', 'col'), may hold values from -3 to 3
Outputs:
- grad_in: bfloat16 [2048, 16384], P('col', 'row')
- new_weight: bfloat16 [16384, 16384], P('row', 'col')
- new_momentum: bfloat16 [16384, 16384], P('row', 'col')
All inputs are finite; a program needn't handle non-finite values.
Results may differ from a plain program's by a relative error of at most 0.014.
Values may be sent and summed in bfloat16 or wider, within the bound.
A program may use at most 128 MiB of HBM per device.

v0:
```python
import jax
import jax.numpy as jnp
from jax import lax
from jax.sharding import PartitionSpec as P


def shards(attn, grad_out, weight, momentum):
    contract_rows = (((0,), (0,)), ((), ()))
    contract_cols = (((1,), (1,)), ((), ()))
    grads_all = lax.all_gather(grad_out, "row", axis=0, tiled=True)
    rows_here = grads_all
    grad_w = lax.dot_general(
        lax.all_gather(attn, "col", axis=0, tiled=True),
        rows_here,
        contract_rows,
        preferred_element_type=jnp.float32,
    )
    rows_here = grads_all
    grad_in = lax.psum_scatter(
        lax.dot_general(
            rows_here, weight, contract_cols, preferred_element_type=jnp.float32
        ).astype(jnp.bfloat16),
        "col",
        scatter_dimension=0,
        tiled=True,
    )
    mom = 0.9 * momentum.astype(jnp.float32) + grad_w
    new_weight = (weight.astype(jnp.float32) - 0.25 * mom).astype(jnp.bfloat16)
    return (grad_in, new_weight, mom.astype(jnp.bfloat16))


def solution(mesh):
    in_specs = (P("col", "row"), P("row", "col"), P("row", "col"), P("row", "col"))
    out_specs = (P("col", "row"), P("row", "col"), P("row", "col"))
    return jax.shard_map(shards, mesh=mesh, in_specs=in_specs, out_specs=out_specs, check_vma=False)
```

profile of v0, /device:TPU:0, one launch (start us, length us, event | category | flops | bytes accessed | tf_op | source)
XLA Modules:
  0.0 164.3 jit_solution(2336899763222875752)
XLA Ops:
  7.2 0.0 all-gather.3.cloned.1.call-start
  7.2 0.7 all-gather.3.cloned.1.call-update
  7.9 0.0 all-gather.5.cloned.1.call-start
  7.9 0.7 all-gather.5.cloned.1.call-update
  8.6 0.0 reduce-scatter.2.cloned.1.call-start
  8.7 74.9 %all-gather.3.cloned.1.call-done = bf16[2048,2048]{1,0:T(8,128)(2,1)} async-done(((bf16[128,2048]{1,0:T(8,128)(2,1)}), bf16[2048,2048]{1,0:T(8,128)(2,1)}) %all-gather.3.cloned.1.call-update) | async-done | bytes 8388624 | tf_op jit(solution)/shard_map/all_gather | solution.py:10
  83.6 13.8 %convolution_convert_fusion = bf16[2048,1024]{1,0:T(8,128)(2,1)} fusion(bf16[2048,2048]{1,0:T(8,128)(2,1)} %all-gather.3.cloned.1.call-done, bf16[1024,2048]{1,0:T(8,128)(2,1)} %param.6), kind=kOutput, calls=%fused_computation.3 | convolution fusion | flops 8592031744 | bytes 16777216 | tf_op jit(solution)/shard_map/dot_general | solution.py:20
  97.4 0.0 reduce-scatter.2.cloned.1.call-update
  97.4 19.5 %all-gather.5.cloned.1.call-done = bf16[2048,1024]{1,0:T(8,128)(2,1)} async-done(((bf16[256,1024]{1,0:T(8,128)(2,1)}), bf16[2048,1024]{1,0:T(8,128)(2,1)}) %all-gather.5.cloned.1.call-update) | async-done | bytes 4194320 | tf_op jit(solution)/shard_map/all_gather | solution.py:13
  117.0 17.7 %fusion = (bf16[1024,2048]{1,0:T(8,128)(2,1)}, bf16[1024,2048]{1,0:T(8,128)(2,1)}) fusion(bf16[1024,2048]{1,0:T(8,128)(2,1)} %param.7, bf16[1024,2048]{1,0:T(8,128)(2,1)} %param.6, bf16[2048,1024]{1,0:T(8,128)(2,1)} %all-gather.5.cloned.1.call-done, bf16[2048,2048]{1,0:T(8,128)(2,1)} %all-gather.3.cloned.1.call-done), kind=kOutput, calls=%fused_computation.2 | convolution fusion | flops 8606711808 | bytes 29360128 | tf_op jit(solution)/shard_map/dot_general | solution.py:12
  134.7 23.1 %reduce-scatter.2.cloned.1.call-done = bf16[256,1024]{1,0:T(8,128)(2,1)} async-done(((bf16[2048,1024]{1,0:T(8,128)(2,1)}), bf16[256,1024]{1,0:T(8,128)(2,1)}) %reduce-scatter.2.cloned.1.call-update) | async-done | bytes 524304 | tf_op jit(solution)/shard_map/reduce_scatter | solution.py:19
Async XLA Ops:
  7.2 76.4 %all-gather.3.cloned.1.call-start = ((), (), s32[]{:S(2)}) async-start(), calls=%async_computation.1 | async-start | bytes 8912896 | tf_op jit(solution)/shard_map/all_gather | solution.py:10
  7.9 109.1 %all-gather.5.cloned.1.call-start = ((), (), s32[]{:S(2)}) async-start(), calls=%async_computation.3 | async-start | bytes 4718592 | tf_op jit(solution)/shard_map/all_gather | solution.py:13
  8.6 149.2 %reduce-scatter.2.cloned.1.call-start = ((), (), s32[]{:S(2)}) async-start(), calls=%async_computation.2 | async-start | bytes 4718592 | tf_op jit(solution)/shard_map/reduce_scatter | solution.py:19
Sparse Core Ops, SparseCore 0:
  10.1 73.4 all-gather.2
  85.3 31.6 all-gather.4
  119.9 37.8 reduce-scatter.1
where the time goes:
time: 164 us
  waiting for transfers between devices  119 us (73%)
  matrix products  31.6 us (19%)
  between operations  13.7 us (8%)
    all_gather x1, waiting for transfers between devices, shards(): grads_all = lax.all_gather(grad_out, 'row', axis=0, tiled=True)  74.9 us
    reduce_scatter x1, waiting for transfers between devices, shards(): lax.psum_scatter(lax.dot_general(rows_here, weight, contract_cols, prefer...  23.1 us
    all_gather x1, waiting for transfers between devices, shards(): lax.all_gather(attn, 'col', axis=0, tiled=True)  19.5 us
    dot_general x1, matrix products, shards(): lax.dot_general(lax.all_gather(attn, 'col', axis=0, tiled=True), rows_her...  17.7 us
    dot_general x1, matrix products, shards(): lax.dot_general(rows_here, weight, contract_cols, preferred_element_type=...  13.8 us
  transfers between devices with their start and end apart: 3, of which 3 were waited for; matrix products, arithmetic and copies ran while one was open for 19% of the time, Pallas kernels for 0%

commit v1 on v0

--- a/solution.py
+++ b/solution.py
@@ -7,7 +7,9 @@
 def shards(attn, grad_out, weight, momentum):
     contract_rows = (((0,), (0,)), ((), ()))
     contract_cols = (((1,), (1,)), ((), ()))
-    grads_all = lax.all_gather(grad_out, "row", axis=0, tiled=True)
+    grads_all = jnp.concatenate(
+        lax.all_to_all(jnp.stack([grad_out] * lax.axis_size("row")), "row", 0, 0), axis=0
+    )
     rows_here = grads_all
     grad_w = lax.dot_general(
         lax.all_gather(attn, "col", axis=0, tiled=True),

time: 164 us -> 231 us (1.41)
  waiting for transfers between devices: 119 us -> 172 us
  starting transfers between devices: 0.11 us -> 8.12 us
  local copies, waits for them, and re-layouts: 0 us -> 5.34 us
    all_to_all x0 -> x1, waiting for transfers between devices: none -> 147 us  [shards(): lax.all_to_all(jnp.stack([grad_out] * lax.axis_size('row')), 'row', 0, 0)]
    all_gather x1 -> x0, waiting for transfers between devices: 74.9 us -> none  [shards(): grads_all = lax.all_gather(grad_out, 'row', axis=0, tiled=True)]
    all_gather x1, waiting for transfers between devices: 19.5 us -> 0.02 us  [shards(): lax.all_gather(attn, 'col', axis=0, tiled=True)]
    all_to_all x0 -> x1, starting transfers between devices: none -> 8.04 us  [shards(): lax.all_to_all(jnp.stack([grad_out] * lax.axis_size('row')), 'row', 0, 0)]
    another operation x0 -> x1, local copies, waits for them, and re-layouts: none -> 5.34 us  [shards(): jnp.stack([grad_out] * lax.axis_size('row'))]
  transfers between devices with their start and end apart: 3 -> 3, of which waited for: 3 -> 2; matrix products, arithmetic and copies ran while one was open for 19% -> 14% of each run, Pallas kernels for 0% -> 0%
where the time goes in v1:
time: 231 us
  waiting for transfers between devices  172 us (74%)
  matrix products  31.6 us (14%)
  between operations  14.1 us (6%)
  starting transfers between devices  8.12 us (4%)
  local copies, waits for them, and re-layouts  5.34 us (2%)
    all_to_all x1, waiting for transfers between devices, shards(): lax.all_to_all(jnp.stack([grad_out] * lax.axis_size('row')), 'row', 0, 0)  147 us
    reduce_scatter x1, waiting for transfers between devices, shards(): lax.psum_scatter(lax.dot_general(rows_here, weight, contract_cols, prefer...  24.1 us
    dot_general x1, matrix products, shards(): lax.dot_general(lax.all_gather(attn, 'col', axis=0, tiled=True), rows_her...  17.7 us
    dot_general x1, matrix products, shards(): lax.dot_general(rows_here, weight, contract_cols, preferred_element_type=...  13.9 us
    all_to_all x1, starting transfers between devices, shards(): lax.all_to_all(jnp.stack([grad_out] * lax.axis_size('row')), 'row', 0, 0)  8.04 us
    another operation x1, local copies, waits for them, and re-layouts, shards(): jnp.stack([grad_out] * lax.axis_size('row'))  5.34 us
  transfers between devices with their start and end apart: 3, of which 2 were waited for; matrix products, arithmetic and copies ran while one was open for 14% of the time, Pallas kernels for 0%

profile of v1, /device:TPU:0, one launch (start us, length us, event | category | flops | bytes accessed | tf_op | source)
XLA Modules:
  0.0 230.7 jit_solution(1454349569333646557)
XLA Ops:
  7.2 5.3 %stack.2 = bf16[16,128,2048]{2,1,0:T(8,128)(2,1)} broadcast(bf16[128,2048]{1,0:T(8,128)(2,1)} %param.5), dimensions={1,2} | broadcast | bytes 8912896 | tf_op jit(solution)/shard_map/stack | solution.py:11
  12.5 8.0 %all-to-all-start = ((bf16[16,128,2048]{2,1,0:T(8,128)(2,1)}), bf16[16,128,2048]{2,1,0:T(8,128)(2,1)}, u32[]{:S(2)}, u32[]{:S(2)}) async-start(bf16[16,128,2048]{2,1,0:T(8,128)(2,1)} %stack.2), calls=%async_computation | async-start | bytes 16777216 | tf_op jit(solution)/shard_map/all_to_all | solution.py:11
  20.5 0.0 all-gather.2.cloned.1.call-start
  20.6 0.7 all-gather.2.cloned.1.call-update
  21.3 0.0 reduce-scatter.2.cloned.1.call-start
  21.3 146.8 %all-to-all-done = bf16[16,128,2048]{2,1,0:T(8,128)(2,1)} async-done(((bf16[16,128,2048]{2,1,0:T(8,128)(2,1)}), bf16[16,128,2048]{2,1,0:T(8,128)(2,1)}, u32[]{:S(2)}, u32[]{:S(2)}) %all-to-all-start) | async-done | bytes 8388640 | tf_op jit(solution)/shard_map/all_to_all | solution.py:11
  168.1 13.9 %convolution_convert_fusion = bf16[2048,1024]{1,0:T(8,128)(2,1)} fusion(bf16[2048,2048]{1,0:T(8,128)(2,1)} %bitcast, bf16[1024,2048]{1,0:T(8,128)(2,1)} %param.6), kind=kOutput, calls=%fused_computation.3 | convolution fusion | flops 8592031744 | bytes 16777216 | tf_op jit(solution)/shard_map/dot_general | solution.py:22
  182.0 0.0 reduce-scatter.2.cloned.1.call-update
  182.0 0.0 all-gather.2.cloned.1.call-done
  182.0 17.7 %fusion = (bf16[1024,2048]{1,0:T(8,128)(2,1)}, bf16[1024,2048]{1,0:T(8,128)(2,1)}) fusion(bf16[1024,2048]{1,0:T(8,128)(2,1)} %param.7, bf16[1024,2048]{1,0:T(8,128)(2,1)} %param.6, bf16[2048,1024]{1,0:T(8,128)(2,1)} %all-gather.2.cloned.1.call-done, bf16[2048,2048]{1,0:T(8,128)(2,1)} %bitcast), kind=kOutput, calls=%fused_computation.2 | convolution fusion | flops 8606711808 | bytes 29360128 | tf_op jit(solution)/shard_map/dot_general | solution.py:14
  199.8 24.1 %reduce-scatter.2.cloned.1.call-done = bf16[256,1024]{1,0:T(8,128)(2,1)} async-done(((bf16[2048,1024]{1,0:T(8,128)(2,1)}), bf16[256,1024]{1,0:T(8,128)(2,1)}) %reduce-scatter.2.cloned.1.call-update) | async-done | bytes 524304 | tf_op jit(solution)/shard_map/reduce_scatter | solution.py:21
Async XLA Ops:
  12.5 155.6 %all-to-all-start = ((bf16[16,128,2048]{2,1,0:T(8,128)(2,1)}), bf16[16,128,2048]{2,1,0:T(8,128)(2,1)}, u32[]{:S(2)}, u32[]{:S(2)}) async-start(bf16[16,128,2048]{2,1,0:T(8,128)(2,1)} %stack.2), calls=%async_computation | async-start | bytes 16777216 | tf_op jit(solution)/shard_map/all_to_all | solution.py:11
  20.5 161.5 %all-gather.2.cloned.1.call-start = ((), (), s32[]{:S(2)}) async-start(), calls=%async_computation.3 | async-start | bytes 4718592 | tf_op jit(solution)/shard_map/all_gather | solution.py:15
  21.3 202.6 %reduce-scatter.2.cloned.1.call-start = ((), (), s32[]{:S(2)}) async-start(), calls=%async_computation.2 | async-start | bytes 4718592 | tf_op jit(solution)/shard_map/reduce_scatter | solution.py:21
Sparse Core Ops, SparseCore 0:
  23.1 33.7 all-gather.1
  182.1 41.7 reduce-scatter.1
